TPU v7x, 32 devices: a whole 2x2x4 slice. The times are simulated.
32 devices in a mesh: dom: 32 (over z, y, x, core).
Axes of the slice: x: 2, y: 2, z: 4, core: 2. Of those that a mesh axis runs over, the one named last changes fastest.
Arguments:
- feats: bfloat16 [131072, 512], P('dom'), may hold values from -6 to 6
- w_self: bfloat16 [512, 512], replicated, may hold values from -0.25 to 0.25
- w_neigh: bfloat16 [512, 512], replicated, may hold values from -0.25 to 0.25
- bias: float32 [512], replicated, may hold values from -1 to 1
- local_tiles: bfloat16 [1024, 3, 128, 128], P('dom'), may hold values from -0.15625 to 0.15625
- local_src: int32 [1024, 3], P('dom'), may hold values from 0 to 31
- local_cnt: int32 [1024], P('dom'), may hold values from 1 to 3
- halo_send: int32 [32, 32], P('dom'), may hold values from 0 to 31
- halo_dst: int32 [32, 32], P('dom'), may hold values from 0 to 31
- halo_tiles: bfloat16 [32, 32, 128, 128], P('dom'), may hold values from -0.15625 to 0.15625
- push_src: int32 [32, 32], P('dom'), may hold values from 0 to 31
- push_dst: int32 [32, 32], P('dom'), may hold values from 0 to 31
- push_tiles: bfloat16 [32, 32, 128, 128], P('dom'), may hold values from -0.15625 to 0.15625
- cotangent: bfloat16 [131072, 512], P('dom'), may hold values from -6 to 6
Outputs:
- hidden_out: bfloat16 [131072, 512], P('dom')
- grad_self: float32 [512, 512], replicated
- grad_neigh: float32 [512, 512], replicated
- grad_bias: float32 [512], replicated
All inputs are finite; a program needn't handle non-finite values.
Results may differ from a plain program's by a relative error of at most 0.007.
Values may be sent and summed in bfloat16 or wider, within the bound.
A program may use at most 320 MiB of HBM per device.

v0:
```python
import jax
import jax.numpy as jnp
from jax import lax
from jax.sharding import PartitionSpec as P


def scatter_pushed(values, targets, local_blocks):
    one_hot = (targets[None, :] == jnp.arange(local_blocks)[:, None]).astype(jnp.bfloat16)
    summed = jnp.dot(
        one_hot, values.reshape(values.shape[0], -1), preferred_element_type=jnp.float32
    )
    return summed.reshape(local_blocks, values.shape[1], values.shape[2])


def shards(
    feats,
    w_self,
    w_neigh,
    bias,
    local_tiles,
    local_src,
    local_cnt,
    halo_send,
    halo_dst,
    halo_tiles,
    push_src,
    push_dst,
    push_tiles,
    cotangent,
):
    block_rows = local_tiles.shape[2]
    width = feats.shape[1]
    slot_count = local_tiles.shape[1]
    local_blocks = feats.shape[0] // block_rows
    blocks = feats.reshape(local_blocks, block_rows, width)
    gathered = blocks[local_src]
    keep_mask = (jnp.arange(slot_count)[None, :] < local_cnt[:, None]).astype(jnp.bfloat16)
    masked = local_tiles * keep_mask[:, :, None, None]
    agg_sum = jnp.einsum("bjik,bjkh->bih", masked, gathered, preferred_element_type=jnp.float32)
    outgoing = blocks[halo_send[0]]
    push_in = blocks[push_src[0]]
    partial_sent = jnp.einsum(
        "sik,skh->sih", push_tiles[0], push_in, preferred_element_type=jnp.float32
    ).astype(jnp.bfloat16)
    arrived = lax.all_to_all(outgoing, "dom", split_axis=0, concat_axis=0, tiled=True)
    partials, dest_arrived = (
        lax.all_to_all(partial_sent, "dom", split_axis=0, concat_axis=0, tiled=True),
        lax.all_to_all(push_dst[0], "dom", split_axis=0, concat_axis=0, tiled=True),
    )
    halo_part = jnp.einsum(
        "qik,qkh->qih", halo_tiles[0], arrived, preferred_element_type=jnp.float32
    )
    agg_sum = agg_sum.at[halo_dst[0]].add(halo_part)
    agg_sum = agg_sum + scatter_pushed(partials, dest_arrived, local_blocks)
    agg = agg_sum.astype(jnp.bfloat16).reshape(local_blocks * block_rows, width)
    pre = (
        jnp.dot(feats, w_self, preferred_element_type=jnp.float32)
        + jnp.dot(agg, w_neigh, preferred_element_type=jnp.float32)
        + bias
    )
    sigma = jax.nn.sigmoid(pre)
    hidden_out = (pre * sigma).astype(jnp.bfloat16)
    dpre = (cotangent.astype(jnp.float32) * sigma * (1.0 + pre * (1.0 - sigma))).astype(
        jnp.bfloat16
    )
    term_self = jnp.dot(feats.T, dpre, preferred_element_type=jnp.float32)
    term_neigh = jnp.dot(agg.T, dpre, preferred_element_type=jnp.float32)
    term_bias = jnp.sum(dpre.astype(jnp.float32), axis=0)
    grad_self, grad_neigh, grad_bias = lax.psum((term_self, term_neigh, term_bias), "dom")
    return (hidden_out, grad_self, grad_neigh, grad_bias)


def solution(mesh):
    placed = (
        P("dom", None),
        P(),
        P(),
        P(),
        P("dom", None, None, None),
        P("dom", None),
        P("dom"),
        P("dom", None),
        P("dom", None),
        P("dom", None, None, None),
        P("dom", None),
        P("dom", None),
        P("dom", None, None, None),
        P("dom", None),
    )
    return jax.shard_map(
        shards,
        mesh=mesh,
        in_specs=placed,
        out_specs=(P("dom", None), P(), P(), P()),
        check_vma=False,
    )
```

profile of v0, /device:TPU:0, one launch (start us, length us, event | category | flops | bytes accessed | tf_op | source)
XLA Modules:
  0.0 442.8 jit_solution(14998779571770807329)
XLA Ops:
  7.2 0.0 copy-start
  7.2 1.4 copy.40
  8.6 7.3 %all-to-all-start = ((s32[32,1,1]{2,1,0:T(1,128)}), s32[32,1,1]{2,1,0:T(1,128)S(1)}, u32[]{:S(2)}, u32[]{:S(2)}) async-start(s32[32,1,1]{2,1,0:T(1,128)} %copy.40), calls=%async_computation | async-start | bytes 32768 | tf_op jit(solution)/shard_map/all_to_all | solution.py:48
  15.9 0.7 fusion.11
  16.6 5.0 %gather_fusion.1 = bf16[32,128,512]{2,1,0:T(8,128)(2,1)} fusion(bf16[32,128,512]{2,1,0:T(8,128)(2,1)} %bitcast.57, s32[1024]{0:T(1024)S(1)} %pad_clamp_fusion.1), kind=kCustom, calls=%fused_computation.1 | custom fusion | bytes 8388736 | tf_op jit(solution)/shard_map/gather | solution.py:41
  21.6 0.0 copy-done
  21.6 5.5 %convert_bitcast_fusion = bf16[32,128,512]{1,2,0:T(8,128)(2,1)} fusion(bf16[32,128,512]{2,1,0:T(8,128)(2,1)} %gather_fusion.1, bf16[1,32,128,128]{3,2,1,0:T(8,128)(2,1)S(1)} %copy-done), kind=kOutput, calls=%fused_computation.13 | convolution fusion | flops 538968064 | bytes 9437184 | tf_op jit(solution)/shard_map/sik,skh->sih/dot_general | solution.py:42
  27.1 0.0 all-to-all-done
  27.1 6.0 %all-to-all-start.1 = ((bf16[32,128,512]{1,2,0:T(8,128)(2,1)}), bf16[32,128,512]{1,2,0:T(8,128)(2,1)}, u32[]{:S(2)}, u32[]{:S(2)}) async-start(bf16[32,128,512]{1,2,0:T(8,128)(2,1)} %convert_bitcast_fusion), calls=%async_computation.1 | async-start | bytes 8388608 | tf_op jit(solution)/shard_map/all_to_all | solution.py:47
  33.1 0.0 copy-done.11
  33.1 5.0 %gather_fusion.2 = bf16[32,128,512]{2,1,0:T(8,128)(2,1)} fusion(bf16[32,128,512]{2,1,0:T(8,128)(2,1)} %bitcast.58, s32[1024]{0:T(1024)S(1)} %pad_clamp_fusion), kind=kCustom, calls=%fused_computation.2 | custom fusion | bytes 8388736 | tf_op jit(solution)/shard_map/gather | solution.py:40
  38.1 6.5 %copy.45 = bf16[32,128,512]{1,2,0:T(8,128)(2,1)} copy(bf16[32,128,512]{2,1,0:T(8,128)(2,1)} %gather_fusion.2) | data formatting | bytes 8388608 | tf_op jit(solution)/shard_map/gather | solution.py:40
  44.6 82.4 %all-to-all-done.1 = bf16[32,128,512]{1,2,0:T(8,128)(2,1)} async-done(((bf16[32,128,512]{1,2,0:T(8,128)(2,1)}), bf16[32,128,512]{1,2,0:T(8,128)(2,1)}, u32[]{:S(2)}, u32[]{:S(2)}) %all-to-all-start.1) | async-done | bytes 4194336 | tf_op jit(solution)/shard_map/all_to_all | solution.py:47
  126.9 4.1 all-to-all-start.2
  131.0 0.0 all-reduce.3.cloned.1.call-start
  131.1 0.0 copy-done.6
  131.1 0.1 copy.39
  131.2 0.1 reshape.136
  131.3 0.0 copy-start.12
  131.3 0.0 copy-start.7
  131.3 0.0 copy-start.5
  131.3 9.1 %gather_fusion = bf16[96,128,512]{2,1,0:T(8,128)(2,1)} fusion(bf16[32,128,512]{2,1,0:T(8,128)(2,1)} %bitcast.59, s32[1024]{0:T(1024)S(1)} %pad_clamp_fusion.2), kind=kCustom, calls=%fused_computation | custom fusion | bytes 25166208 | tf_op jit(solution)/shard_map/gather | solution.py:36
  140.4 0.0 copy-done.12
  140.4 0.0 copy-done.7
  140.5 0.1 fusion.7
  140.5 0.0 copy-done.5
  140.5 7.7 %fusion.14 = f32[4096,512]{1,0:T(8,128)} fusion(bf16[4096,512]{1,0:T(8,128)(2,1)} %param.14, bf16[512,512]{1,0:T(8,128)(2,1)S(1)} %copy-done.5), kind=kOutput, calls=%fused_computation.35 | convolution fusion | flops 2147483648 | bytes 13107200 | tf_op jit(solution)/shard_map/dot_general | solution.py:57
  148.3 0.7 reduce
  148.9 7.9 %copy.51 = bf16[4,8,128,512]{3,1,2,0:T(8,128)(2,1)} copy(bf16[4,8,128,512]{2,3,1,0:T(8,128)(2,1)} %bitcast.41) | data formatting | bytes 8388608
  156.9 68.0 %all-to-all-done.2 = bf16[32,128,512]{1,2,0:T(8,128)(2,1)} async-done(((bf16[32,128,512]{1,2,0:T(8,128)(2,1)}), bf16[32,128,512]{1,2,0:T(8,128)(2,1)}, u32[]{:S(2)}, u32[]{:S(2)}) %all-to-all-start.2) | async-done | bytes 4194336 | tf_op jit(solution)/shard_map/all_to_all | solution.py:45
  224.9 0.0 copy-done.4
  224.9 6.8 %convolution_bitcast_fusion = f32[32,128,512]{1,2,0:T(8,128)} fusion(bf16[32,128,512]{1,2,0:T(8,128)(2,1)} %all-to-all-done.2, bf16[1,32,128,128]{3,2,1,0:T(8,128)(2,1)S(1)} %copy-done.4), kind=kOutput, calls=%fused_computation.14 | convolution fusion | flops 536870912 | bytes 13631488 | tf_op jit(solution)/shard_map/qik,qkh->qih/dot_general | solution.py:50
  231.7 9.0 %copy.46 = f32[32,128,512]{2,1,0:T(8,128)} copy(f32[32,128,512]{1,2,0:T(8,128)} %convolution_bitcast_fusion) | data formatting | bytes 16777216 | tf_op jit(solution)/shard_map/qik,qkh->qih/dot_general | solution.py:50
  240.7 3.6 fusion
  244.3 14.5 %bitcast_add_fusion = f32[32,128,512]{2,1,0:T(8,128)} fusion(f32[32,128,512]{2,0,1:T(8,128)S(1)} %fusion, bf16[32,3,128,512]{3,2,1,0:T(8,128)(2,1)} %bitcast.60, bf16[32,3,128,128]{3,2,1,0:T(8,128)(2,1)S(1)} %copy-done.3, bf16[32,3]{1,0:T(8,128)(2,1)S(1)} %fusion.7), kind=kOutput, calls=%fused_computation.4 | convolution fusion | flops 1614282752 | bytes 32506048 | tf_op jit(solution)/shard_map/bjik,bjkh->bih/dot_general | solution.py:39
  258.8 18.4 %scatter_fusion = f32[32,128,512]{2,1,0:T(8,128)} fusion(f32[32,128,512]{2,1,0:T(8,128)} %bitcast_add_fusion, s32[32]{0:T(128)S(1)} %fusion.12, f32[32,128,512]{2,1,0:T(8,128)} %copy.46), kind=kCustom, calls=%fused_computation.3 | custom fusion | flops 2097152 | bytes 25165952 | tf_op jit(solution)/shard_map/scatter-add | solution.py:53
  277.3 4.2 convert_element_type.32
  281.5 0.4 copy-done.8
  281.8 0.1 copy-done.9
  282.0 0.0 copy-done.10
  282.0 8.6 %convert_reduce_fusion = (f32[512]{0:T(512)S(1)}, bf16[4096,512]{1,0:T(8,128)(2,1)S(1)}, bf16[4096,512]{1,0:T(8,128)(2,1)}) fusion(bf16[4096,512]{1,0:T(8,128)(2,1)S(1)} %copy-done.8, f32[512]{0:T(512)S(1)} %copy-done.10, f32[4096,512]{1,0:T(8,128)} %fusion.14, bf16[4096,512]{1,0:T(8,128)(2,1)S(1)} %bitcast.61, bf16[512,512]{1,0:T(8,128)(2,1)S(1)} %copy-done.9), kind=kOutput, calls=%fused_computation.5 | convolution fusion | flops 2181037568 | bytes 25694208 | tf_op jit(solution)/shard_map/dot_general | solution.py:58
  290.5 3.3 fusion.15
  293.9 3.3 convolution_bitcast_fusion.1
  297.2 0.0 all-reduce.3.cloned.1.call-update
  297.2 38.6 %psum.23 = f32[512]{0:T(512)} all-reduce(f32[512]{0:T(512)S(1)} %get-tuple-element.22), channel_id=1, replica_groups=mesh['dom'=32] {'dom'}, use_global_device_ids=true, to_apply=%region_4.0 | all-reduce | flops 512 | bytes 4096 | tf_op jit(solution)/shard_map/psum | solution.py:69
  335.8 95.3 %all-reduce.3.cloned.1.call-done = (f32[512,512]{0,1:T(8,128)}, f32[512,512]{1,0:T(8,128)}) async-done(((f32[512,512]{0,1:T(8,128)}, f32[512,512]{1,0:T(8,128)}), (f32[512,512]{0,1:T(8,128)}, f32[512,512]{1,0:T(8,128)})) %all-reduce.3.cloned.1.call-update) | async-done | bytes 2097168 | tf_op jit(solution)/shard_map/psum | solution.py:69
  431.1 2.5 copy.47
  433.7 2.3 copy.61
  (18 shorter events, 0.1 us)
Async XLA Ops:
  7.2 14.4 %copy-start = (bf16[1,32,128,128]{3,2,1,0:T(8,128)(2,1)S(1)}, bf16[1,32,128,128]{3,2,1,0:T(8,128)(2,1)}, u32[]{:S(2)}) copy-start(bf16[1,32,128,128]{3,2,1,0:T(8,128)(2,1)} %param.26) | copy-start | bytes 3145732
  8.6 18.5 %all-to-all-start = ((s32[32,1,1]{2,1,0:T(1,128)}), s32[32,1,1]{2,1,0:T(1,128)S(1)}, u32[]{:S(2)}, u32[]{:S(2)}) async-start(s32[32,1,1]{2,1,0:T(1,128)} %copy.40), calls=%async_computation | async-start | bytes 32768 | tf_op jit(solution)/shard_map/all_to_all | solution.py:48
  27.1 6.0 %copy-start.11 = (s32[1,32]{1,0:T(1,128)S(1)}, s32[1,32]{1,0:T(1,128)}, u32[]{:S(2)}) copy-start(s32[1,32]{1,0:T(1,128)} %param.21) | copy-start | bytes 388
  27.1 99.8 %all-to-all-start.1 = ((bf16[32,128,512]{1,2,0:T(8,128)(2,1)}), bf16[32,128,512]{1,2,0:T(8,128)(2,1)}, u32[]{:S(2)}, u32[]{:S(2)}) async-start(bf16[32,128,512]{1,2,0:T(8,128)(2,1)} %convert_bitcast_fusion), calls=%async_computation.1 | async-start | bytes 8388608 | tf_op jit(solution)/shard_map/all_to_all | solution.py:47
  44.6 86.5 %copy-start.6 = (s32[32,3]{0,1:T(4,128)S(1)}, s32[32,3]{0,1:T(4,128)}, u32[]{:S(2)}) copy-start(s32[32,3]{0,1:T(4,128)} %param.19) | copy-start | bytes 1156
  126.9 98.0 %all-to-all-start.2 = ((bf16[32,128,512]{1,2,0:T(8,128)(2,1)}), bf16[32,128,512]{1,2,0:T(8,128)(2,1)}, u32[]{:S(2)}, u32[]{:S(2)}) async-start(bf16[32,128,512]{1,2,0:T(8,128)(2,1)} %copy.45), calls=%async_computation.2 | async-start | bytes 8388608 | tf_op jit(solution)/shard_map/all_to_all | solution.py:45
  131.0 300.1 %all-reduce.3.cloned.1.call-start = ((), (), s32[]{:S(2)}) async-start(), calls=%async_computation.3 | async-start | bytes 4194304 | tf_op jit(solution)/shard_map/psum | solution.py:69
  131.3 9.1 %copy-start.12 = (s32[1,32]{1,0:T(1,128)S(1)}, s32[1,32]{1,0:T(1,128)}, u32[]{:S(2)}) copy-start(s32[1,32]{1,0:T(1,128)} %param.22) | copy-start | bytes 388
  131.3 9.1 %copy-start.7 = (s32[32]{0:T(128)S(1)}, s32[32]{0:T(128)}, u32[]{:S(2)}) copy-start(s32[32]{0:T(128)} %param.20) | copy-start | bytes 388
  131.3 9.2 %copy-start.5 = (bf16[512,512]{1,0:T(8,128)(2,1)S(1)}, bf16[512,512]{1,0:T(8,128)(2,1)}, u32[]{:S(2)}) copy-start(bf16[512,512]{1,0:T(8,128)(2,1)} %param.15) | copy-start | bytes 1572868
  148.9 76.0 %copy-start.4 = (bf16[1,32,128,128]{3,2,1,0:T(8,128)(2,1)S(1)}, bf16[1,32,128,128]{3,2,1,0:T(8,128)(2,1)}, u32[]{:S(2)}) copy-start(bf16[1,32,128,128]{3,2,1,0:T(8,128)(2,1)} %param.23) | copy-start | bytes 3145732
  240.7 3.6 copy-start.3
  277.3 4.6 %copy-start.8 = (bf16[4096,512]{1,0:T(8,128)(2,1)S(1)}, bf16[4096,512]{1,0:T(8,128)(2,1)}, u32[]{:S(2)}) copy-start(bf16[4096,512]{1,0:T(8,128)(2,1)} %param.27) | copy-start | bytes 12582916
  277.3 4.7 %copy-start.9 = (bf16[512,512]{1,0:T(8,128)(2,1)S(1)}, bf16[512,512]{1,0:T(8,128)(2,1)}, u32[]{:S(2)}) copy-start(bf16[512,512]{1,0:T(8,128)(2,1)} %param.16) | copy-start | bytes 1572868
  277.3 4.7 %copy-start.10 = (f32[512]{0:T(512)S(1)}, f32[512]{0:T(512)}, u32[]{:S(2)}) copy-start(f32[512]{0:T(512)} %param.17) | copy-start | bytes 6148
  290.5 3.3 copy-start.2
  293.9 142.1 %copy-start.1 = (bf16[1,32,128,128]{3,2,1,0:T(8,128)(2,1)S(1)}, bf16[1,32,128,128]{3,2,1,0:T(8,128)(2,1)}, u32[]{:S(2)}) copy-start(bf16[1,32,128,128]{3,2,1,0:T(8,128)(2,1)} %param.26) | copy-start | bytes 3145732
Sparse Core Ops, SparseCore 0:
  297.3 133.7 all-reduce.2
where the time goes:
time: 444 us; the launch traced here: 443 us
  waiting for transfers between devices  246 us (55%)
  matrix products  53.3 us (12%)
  local copies, waits for them, and re-layouts  49.5 us (11%)
  blocking collectives  38.6 us (9%)
  other arithmetic  24.1 us (5%)
  starting transfers between devices  17.4 us (4%)
  between operations  14.2 us (3%)
    psum x1, waiting for transfers between devices, shards(): lax.psum((term_self, term_neigh, term_bias), 'dom')  95.3 us
    all_to_all x1, waiting for transfers between devices, shards(): lax.all_to_all(partial_sent, 'dom', split_axis=0, concat_axis=0, tiled=True)  82.4 us
    all_to_all x1, waiting for transfers between devices, shards(): lax.all_to_all(outgoing, 'dom', split_axis=0, concat_axis=0, tiled=True)  68 us
    psum x1, blocking collectives, shards(): lax.psum((term_self, term_neigh, term_bias), 'dom')  38.6 us
    scatter-add x1, other arithmetic, shards(): agg_sum = agg_sum.at[halo_dst[0]].add(halo_part)  18.4 us
    dot_general x1, matrix products, shards(): jnp.einsum('bjik,bjkh->bih', masked, gathered, preferred_element_type=jnp...  14.5 us
    unnamed x29, local copies, waits for them, and re-layouts  13.3 us
    gather x2, local copies, waits for them, and re-layouts, shards(): outgoing = blocks[halo_send[0]]  11.5 us
  transfers between devices with their start and end apart: 4, of which 3 were waited for; matrix products, arithmetic and copies ran while one was open for 11% of the time, Pallas kernels for 0%

commit v1 on v0

v1 whole, which is shorter than its diff:
```python
import functools

import jax
import jax.numpy as jnp
from jax import lax
from jax.experimental import pallas as pl
from jax.experimental.pallas import tpu as pltpu
from jax.sharding import PartitionSpec as P

MESH = pl.DeviceIdType.MESH
VMEM_BYTES = 66_000_000
PLANE = 8


def flip(me, mask, n):
    out = 0
    weight = 1
    while weight < n:
        out = out + weight * ((me // weight + mask // weight) % 2)
        weight *= 2
    return out


def greet_all(n, me):
    barrier = pltpu.get_barrier_semaphore()

    def greet(i, carry):
        pl.semaphore_signal(
            barrier, inc=1, device_id=(lax.rem(me + i, n),), device_id_type=MESH
        )
        return carry

    lax.fori_loop(1, n, greet, 0)
    return barrier


def exchange_kernel(
    n,
    send_ids,
    push_ids,
    local_ids,
    keep,
    feats,
    push_tiles,
    local_tiles,
    w_self,
    bias,
    dst_rows,
    halo_in,
    push_in,
    dst_in,
    local_out,
    base_out,
    halo_buf,
    push_buf,
    local_buf,
    base_buf,
    halo_ss,
    halo_rs,
    push_ss,
    push_rs,
    dst_ss,
    dst_rs,
    own_sems,
    out_sems,
):
    me = lax.axis_index("dom")
    blk = push_tiles.shape[1]
    planes = n // PLANE
    barrier = greet_all(n, me)

    def message(i):
        mask = ((i % planes + 1) % planes) * PLANE + i // planes
        return mask, flip(me, mask, n)

    def gather(i, carry):
        _, to = message(i)
        halo_buf[to] = feats[send_ids[0, to]]
        return carry

    lax.fori_loop(0, n, gather, 0)
    pl.semaphore_wait(barrier, n - 1)

    def halo_copy(to):
        return pltpu.make_async_remote_copy(
            halo_buf.at[to], halo_in.at[me], halo_ss, halo_rs, device_id=(to,), device_id_type=MESH
        )

    def push_copy(to):
        return pltpu.make_async_remote_copy(
            push_buf.at[to], push_in.at[me], push_ss, push_rs, device_id=(to,), device_id_type=MESH
        )

    def dst_copy(to):
        return pltpu.make_async_remote_copy(
            dst_rows.at[to], dst_in.at[me], dst_ss, dst_rs, device_id=(to,), device_id_type=MESH
        )

    def first(i, carry):
        mask, to = message(i)

        @pl.when(mask > 0)
        def _():
            halo_copy(to).start()
            dst_copy(to).start()

        push_buf[to] = jnp.dot(
            push_tiles[to], feats[push_ids[0, to]], preferred_element_type=jnp.float32
        ).astype(jnp.bfloat16)
        return carry

    lax.fori_loop(0, n, first, 0)

    def second(i, carry):
        mask, to = message(i)

        @pl.when(mask > 0)
        def _():
            push_copy(to).start()

        return carry

    lax.fori_loop(0, n, second, 0)
    own = (
        pltpu.make_async_copy(halo_buf.at[me], halo_in.at[me], own_sems.at[0]),
        pltpu.make_async_copy(push_buf.at[me], push_in.at[me], own_sems.at[1]),
        pltpu.make_async_copy(dst_rows.at[me], dst_in.at[me], own_sems.at[2]),
    )
    for copy in own:
        copy.start()

    slots = local_tiles.shape[1]

    def local(b, carry):
        total = jnp.zeros(feats.shape[1:], jnp.float32)
        for j in range(slots):
            tile = local_tiles[b, j] * keep[b * slots + j].astype(jnp.bfloat16)
            total += jnp.dot(tile, feats[local_ids[b, j]], preferred_element_type=jnp.float32)
        rows = pl.ds(pl.multiple_of(b * blk, blk), blk)
        local_buf[rows, :] = total
        base_buf[rows, :] = (
            jnp.dot(feats[b], w_self[...], preferred_element_type=jnp.float32) + bias[...]
        )
        return carry

    lax.fori_loop(0, feats.shape[0], local, 0)
    outs = (
        pltpu.make_async_copy(local_buf, local_out, out_sems.at[0]),
        pltpu.make_async_copy(base_buf, base_out, out_sems.at[1]),
    )
    for copy in outs:
        copy.start()
    for copy in own + outs:
        copy.wait()
    for buf, sem in (
        (halo_in, halo_rs),
        (push_in, push_rs),
        (dst_in, dst_rs),
        (halo_buf, halo_ss),
        (push_buf, push_ss),
        (dst_rows, dst_ss),
    ):
        part = buf.at[pl.ds(0, n - 1)]
        pltpu.make_async_copy(part, part, sem).wait()


def exchange(n, send_ids, push_ids, local_ids, keep, feats, push_tiles, local_tiles, w_self, bias, dst_rows):
    blocks, blk, width = feats.shape
    smem = pl.BlockSpec(memory_space=pltpu.SMEM)
    vmem = pl.BlockSpec(memory_space=pltpu.VMEM)
    hbm = pl.BlockSpec(memory_space=pl.ANY)
    dma = pltpu.SemaphoreType.DMA
    return pl.pallas_call(
        functools.partial(exchange_kernel, n),
        out_shape=(
            jax.ShapeDtypeStruct((n, blk, width), jnp.bfloat16),
            jax.ShapeDtypeStruct((n, blk, width), jnp.bfloat16),
            jax.ShapeDtypeStruct(dst_rows.shape, jnp.int32),
            jax.ShapeDtypeStruct((blocks * blk, width), jnp.float32),
            jax.ShapeDtypeStruct((blocks * blk, width), jnp.float32),
        ),
        in_specs=[smem] * 3 + [vmem] * 7,
        out_specs=(hbm,) * 5,
        scratch_shapes=[
            pltpu.VMEM((n, blk, width), jnp.bfloat16),
            pltpu.VMEM((n, blk, width), jnp.bfloat16),
            pltpu.VMEM((blocks * blk, width), jnp.float32),
            pltpu.VMEM((blocks * blk, width), jnp.float32),
        ]
        + [dma] * 6
        + [dma((3,)), dma((2,))],
        compiler_params=pltpu.CompilerParams(
            collective_id=0, has_side_effects=True, vmem_limit_bytes=VMEM_BYTES
        ),
        name="exchange",
    )(send_ids, push_ids, local_ids, keep, feats, push_tiles, local_tiles, w_self, bias, dst_rows)


def dense_kernel(
    steps,
    group,
    halo_dst,
    push_dst,
    halo_in,
    halo_tiles,
    push_in,
    local_part,
    base,
    feats,
    cot,
    w_neigh,
    hidden,
    grads,
    gbias,
    acc,
    gt,
    gb,
):
    i = pl.program_id(0)
    blk = halo_in.shape[1]
    rows, width = feats.shape

    @pl.when(i == 0)
    def _():
        acc[...] = jnp.zeros_like(acc)
        gt[...] = jnp.zeros_like(gt)
        gb[...] = jnp.zeros_like(gb)

    @pl.when(i < steps)
    def _():
        for k in range(group):
            q = i * group + k
            at = pl.ds(pl.multiple_of(halo_dst[q] * blk, blk), blk)
            acc[at, :] += jnp.dot(halo_tiles[k], halo_in[k], preferred_element_type=jnp.float32)
            at = pl.ds(pl.multiple_of(push_dst[q] * blk, blk), blk)
            acc[at, :] += push_in[k].astype(jnp.float32)

    @pl.when(i >= steps)
    def _():
        at = pl.ds(pl.multiple_of((i - steps) * rows, rows), rows)
        agg = (acc[at, :] + local_part[...]).astype(jnp.bfloat16)
        pre = base[...] + jnp.dot(agg, w_neigh[...], preferred_element_type=jnp.float32)
        sigma = jax.nn.sigmoid(pre)
        hidden[...] = (pre * sigma).astype(jnp.bfloat16)
        dpre = (cot[...].astype(jnp.float32) * sigma * (1.0 + pre * (1.0 - sigma))).astype(
            jnp.bfloat16
        )
        gb[...] += jnp.sum(dpre.astype(jnp.float32).reshape(rows // 8, 8, width), axis=0)
        turned = dpre.T
        gt[0] += jnp.dot(turned, feats[...], preferred_element_type=jnp.float32)
        gt[1] += jnp.dot(turned, agg, preferred_element_type=jnp.float32)

    @pl.when(i == pl.num_programs(0) - 1)
    def _():
        grads[pl.ds(0, width), :] = gt[0].T
        grads[pl.ds(width, width), :] = gt[1].T
        gbias[...] = jnp.broadcast_to(jnp.sum(gb[...], axis=0, keepdims=True), gbias.shape)


def dense(halo_dst, push_dst, halo_in, halo_tiles, push_in, local_part, base, feats, cot, w_neigh):
    n, blk, width = halo_in.shape
    nodes = feats.shape[0]
    group, rows = 4, 512
    steps, chunks = n // group, nodes // rows

    def owners(i, *_):
        return (jnp.minimum(i, steps - 1), 0, 0)

    def nodes_at(i, *_):
        return (jnp.maximum(i - steps, 0), 0)

    arrived = pl.BlockSpec((group, blk, width), owners)
    chunk = pl.BlockSpec((rows, width), nodes_at)

    def whole(i, *_):
        return (0, 0)

    return pl.pallas_call(
        functools.partial(dense_kernel, steps, group),
        out_shape=(
            jax.ShapeDtypeStruct((nodes, width), jnp.bfloat16),
            jax.ShapeDtypeStruct((2 * width, width), jnp.float32),
            jax.ShapeDtypeStruct((8, width), jnp.float32),
        ),
        grid_spec=pltpu.PrefetchScalarGridSpec(
            num_scalar_prefetch=2,
            grid=(steps + chunks,),
            in_specs=[
                arrived,
                pl.BlockSpec((group, blk, blk), owners),
                arrived,
                chunk,
                chunk,
                chunk,
                chunk,
                pl.BlockSpec((width, width), whole),
            ],
            out_specs=(
                chunk,
                pl.BlockSpec((2 * width, width), whole),
                pl.BlockSpec((8, width), whole),
            ),
            scratch_shapes=[
                pltpu.VMEM((nodes, width), jnp.float32),
                pltpu.VMEM((2, width, width), jnp.float32),
                pltpu.VMEM((8, width), jnp.float32),
            ],
        ),
        compiler_params=pltpu.CompilerParams(
            dimension_semantics=("arbitrary",), vmem_limit_bytes=VMEM_BYTES
        ),
        name="dense",
    )(halo_dst, push_dst, halo_in, halo_tiles, push_in, local_part, base, feats, cot, w_neigh)


def reduce_kernel(
    n, term, gbias, out, bias_out, acc, send_buf, recv_buf, bias_in, ss, rs, gs, gr, bs, br, own
):
    me = lax.axis_index("dom")
    barrier = greet_all(n, me)
    size = term.shape[0]
    core, second, third = me % 2, (me // 2) % 2, (me // 4) % 2
    bits = [core, second * (1 - core) + third * core, third * (1 - core) + second * core]
    weights = [1, 2 + 2 * core, 4 - 2 * core]
    weight = 8
    while weight < n:
        bits.append((me // weight) % 2)
        weights.append(weight)
        weight *= 2
    partners = [me + (1 - 2 * bit) * w for bit, w in zip(bits, weights)]

    def bias_copy(to):
        return pltpu.make_async_remote_copy(
            gbias, bias_in.at[me], bs, br, device_id=(to,), device_id_type=MESH
        )

    own_bias = pltpu.make_async_copy(gbias, bias_in.at[me], own)
    own_bias.start()
    half = size // 2
    away = pl.multiple_of((1 - bits[0]) * half, half)
    send_buf[pl.ds(0, half), :] = term[pl.ds(away, half), :].astype(jnp.bfloat16)
    pl.semaphore_wait(barrier, n - 1)

    base = 0
    lo = 0
    for step, (bit, partner) in enumerate(zip(bits, partners)):
        half = size // 2
        copy = pltpu.make_async_remote_copy(
            send_buf.at[pl.ds(base, half)],
            recv_buf.at[pl.ds(base, half)],
            ss.at[step],
            rs.at[step],
            device_id=(partner,),
            device_id_type=MESH,
        )
        copy.start()
        if step == 0:

            def greet(i, carry):
                bias_copy(lax.rem(me + i, n)).start()
                return carry

            lax.fori_loop(1, n, greet, 0)
        lo = lo + bit * half
        source = term if step == 0 else acc
        copy.wait()
        if step + 1 < len(bits):
            nxt = half // 2
            bit2 = bits[step + 1]
            away = (1 - bit2) * nxt
            at = pl.multiple_of(lo + away, nxt)
            rel = pl.multiple_of(away, nxt)
            send_buf[pl.ds(base + half, nxt), :] = (
                source[pl.ds(at, nxt), :]
                + recv_buf[pl.ds(pl.multiple_of(base + rel, nxt), nxt), :].astype(jnp.float32)
            ).astype(jnp.bfloat16)
            keep = bit2 * nxt
            at = pl.multiple_of(lo + keep, nxt)
            acc[pl.ds(at, nxt), :] = source[pl.ds(at, nxt), :] + recv_buf[
                pl.ds(pl.multiple_of(base + keep, nxt), nxt), :
            ].astype(jnp.float32)
        else:
            at = pl.multiple_of(lo, half)
            out[pl.ds(at, half), :] = (
                source[pl.ds(at, half), :] + recv_buf[pl.ds(base, half), :].astype(jnp.float32)
            ).astype(jnp.bfloat16)
        base += half
        size = half

    own_bias.wait()
    part = bias_in.at[pl.ds(0, n - 1)]
    pltpu.make_async_copy(part, part, br).wait()
    bias_out[...] = jnp.sum(bias_in[...], axis=0)

    for step in reversed(range(len(bits))):
        at = pl.ds(pl.multiple_of(lo, size), size)
        copy = pltpu.make_async_remote_copy(
            out.at[at],
            out.at[at],
            gs.at[step],
            gr.at[step],
            device_id=(partners[step],),
            device_id_type=MESH,
        )
        copy.start()
        copy.wait()
        lo = lo - bits[step] * size
        size *= 2
    part = bias_in.at[pl.ds(0, n - 1)]
    pltpu.make_async_copy(part, part, bs).wait()


def reduce(n, term, gbias):
    size, width = term.shape
    steps = n.bit_length() - 1
    vmem = pl.BlockSpec(memory_space=pltpu.VMEM)
    dma = pltpu.SemaphoreType.DMA
    return pl.pallas_call(
        functools.partial(reduce_kernel, n),
        out_shape=(
            jax.ShapeDtypeStruct((size, width), jnp.bfloat16),
            jax.ShapeDtypeStruct(gbias.shape, jnp.float32),
        ),
        in_specs=[vmem, vmem],
        out_specs=(vmem, vmem),
        scratch_shapes=[
            pltpu.VMEM((size, width), jnp.float32),
            pltpu.VMEM((size, width), jnp.bfloat16),
            pltpu.VMEM((size, width), jnp.bfloat16),
            pltpu.VMEM((n,) + gbias.shape, jnp.float32),
            dma((steps,)),
            dma((steps,)),
            dma((steps,)),
            dma((steps,)),
            dma,
            dma,
            dma,
        ],
        compiler_params=pltpu.CompilerParams(
            collective_id=1, has_side_effects=True, vmem_limit_bytes=VMEM_BYTES
        ),
        name="reduce_grads",
    )(term, gbias)


def shards(
    n,
    feats,
    w_self,
    w_neigh,
    bias,
    local_tiles,
    local_src,
    local_cnt,
    halo_send,
    halo_dst,
    halo_tiles,
    push_src,
    push_dst,
    push_tiles,
    cotangent,
):
    width = feats.shape[1]
    live = jnp.arange(local_tiles.shape[1])[None, :] < local_cnt[:, None]
    keep = jnp.broadcast_to(live.astype(jnp.float32).reshape(-1, 1, 1), (live.size, 1, 128))
    dst_rows = jnp.broadcast_to(push_dst[0][:, None, None], (n, 8, 128))
    halo_in, push_in, dst_in, local_part, base = exchange(
        n,
        halo_send,
        push_src,
        local_src,
        keep,
        feats.reshape(-1, push_tiles.shape[2], width),
        push_tiles[0],
        local_tiles,
        w_self,
        bias[None, :],
        dst_rows,
    )
    hidden_out, term, term_bias = dense(
        halo_dst[0],
        dst_in[:, 0, 0],
        halo_in,
        halo_tiles[0],
        push_in,
        local_part,
        base,
        feats,
        cotangent,
        w_neigh,
    )
    grads, gbias = reduce(n, term, term_bias)
    grads = grads.astype(jnp.float32)
    return (hidden_out, grads[:width], grads[width:], gbias[0])


def solution(mesh):
    placed = (
        P("dom", None),
        P(),
        P(),
        P(),
        P("dom", None, None, None),
        P("dom", None),
        P("dom"),
        P("dom", None),
        P("dom", None),
        P("dom", None, None, None),
        P("dom", None),
        P("dom", None),
        P("dom", None, None, None),
        P("dom", None),
    )
    return jax.shard_map(
        functools.partial(shards, mesh.shape["dom"]),
        mesh=mesh,
        in_specs=placed,
        out_specs=(P("dom", None), P(), P(), P()),
        check_vma=False,
    )
```

time: 444 us -> 281 us (0.63)
  Pallas kernels: 0 us -> 269 us
  waiting for transfers between devices: 246 us -> 0 us
  matrix products: 53.3 us -> 0 us
  local copies, waits for them, and re-layouts: 49.5 us -> 9.88 us
  blocking collectives: 38.6 us -> 0 us
  other arithmetic: 24.1 us -> 0.73 us
  starting transfers between devices: 17.4 us -> 0 us
  between operations: 14.2 us -> 0.66 us
    pallas_call x0 -> x3, Pallas kernels: none -> 269 us  [the longest x1 196 us: exchange(): pl.pallas_call(functools.partial(exchange_kernel, n), out_shape=(jax.Shap...]
    all_to_all x3 -> x0, waiting for transfers between devices: 150 us -> none  [the longest x1 82.4 us: shards(): lax.all_to_all(partial_sent, 'dom', split_axis=0, concat_axis=0, tiled=True)]
    psum x1 -> x0, waiting for transfers between devices: 95.3 us -> none  [shards(): lax.psum((term_self, term_neigh, term_bias), 'dom')]
    dot_general x8 -> x0, matrix products: 53.3 us -> none  [the longest x1 14.5 us: shards(): jnp.einsum('bjik,bjkh->bih', masked, gathered, preferred_element_type=jnp...]
    psum x1 -> x0, blocking collectives: 38.6 us -> none  [shards(): lax.psum((term_self, term_neigh, term_bias), 'dom')]
    gather x4 -> x0, local copies, waits for them, and re-layouts: 25.6 us -> none  [the longest x2 11.5 us: shards(): outgoing = blocks[halo_send[0]]]
    scatter-add x1 -> x0, other arithmetic: 18.4 us -> none  [shards(): agg_sum = agg_sum.at[halo_dst[0]].add(halo_part)]
    all_to_all x3 -> x0, starting transfers between devices: 17.4 us -> none  [the longest x1 7.3 us: shards(): lax.all_to_all(push_dst[0], 'dom', split_axis=0, concat_axis=0, tiled=True)]
  transfers between devices with their start and end apart: 4 -> 0, of which waited for: 3 -> 0; matrix products, arithmetic and copies ran while one was open for 11% -> 0% of each run, Pallas kernels for 0% -> 0%
where the time goes in v1:
time: 281 us
  Pallas kernels  269 us (96%)
  local copies, waits for them, and re-layouts  9.88 us (4%)
    pallas_call x1, Pallas kernels, exchange(): pl.pallas_call(functools.partial(exchange_kernel, n), out_shape=(jax.Shap...  196 us
    pallas_call x1, Pallas kernels, reduce(): pl.pallas_call(functools.partial(reduce_kernel, n), out_shape=(jax.ShapeD...  47.5 us
    pallas_call x1, Pallas kernels, dense(): pl.pallas_call(functools.partial(dense_kernel, steps, group), out_shape=(...  25.7 us

profile of v1, /device:TPU:0, one launch (start us, length us, event | category | flops | bytes accessed | tf_op | source)
XLA Modules:
  0.0 280.7 jit_solution(17465062187145276974)
XLA Ops:
  0.6 1.4 copy.19.local_ids
  2.0 0.7 fusion
  2.7 0.1 reshape.34
  2.8 0.8 broadcast_in_dim.8.keep
  3.6 1.4 broadcast_in_dim.20.dst_rows
  5.0 196.2 %exchange.1 = (bf16[32,128,512]{2,1,0:T(8,128)(2,1)}, bf16[32,128,512]{2,1,0:T(8,128)(2,1)}, s32[32,8,128]{2,1,0:T(8,128)}, f32[4096,512]{1,0:T(8,128)}, f32[4096,512]{1,0:T(8,128)}) custom-call(s32[1,32]{1,0:T(1,128)} %send_ids.1, s32[1,32]{1,0:T(1,128)} %push_ids.1, s32[32,3]{1,0:T(8,128)} %copy.19.local_ids, f32[96,1,128]{2,1,0:T(1,128)} %broadcast_in_dim.8.keep, ...), custom_call_target="tpu_custom_call" | custom-call | tf_op jit(solution)/shard_map/exchange/pallas_call | solution.py:173
  201.2 2.1 slice_reduce_fusion.push_dst
  203.3 25.7 %dense.1 = (bf16[4096,512]{1,0:T(8,128)(2,1)}, f32[1024,512]{1,0:T(8,128)}, f32[8,512]{1,0:T(8,128)}) custom-call(s32[32]{0:T(128)} %bitcast.13, s32[32]{0:T(128)} %slice_reduce_fusion.push_dst, bf16[32,128,512]{2,1,0:T(8,128)(2,1)} %get-tuple-element.15.halo_in, bf16[32,128,128]{2,1,0:T(8,128)(2,1)} %bitcast.8, ...), custom_call_target="tpu_custom_call" | custom-call | tf_op jit(solution)/shard_map/dense/pallas_call | solution.py:278
  229.1 47.5 %reduce_grads.1 = (bf16[1024,512]{1,0:T(8,128)(2,1)}, f32[8,512]{1,0:T(8,128)}) custom-call(f32[1024,512]{1,0:T(8,128)} %get-tuple-element.20.term, f32[8,512]{1,0:T(8,128)} %get-tuple-element.21.gbias), custom_call_target="tpu_custom_call" | custom-call | tf_op jit(solution)/shard_map/reduce_grads/pallas_call | solution.py:418
  276.6 1.3 slice.15
  277.9 2.8 fusion.1

commit v2 on v1

--- a/solution.py
+++ b/solution.py
@@ -39,13 +39,13 @@
     send_ids,
     push_ids,
     local_ids,
-    keep,
+    local_cnt,
     feats,
     push_tiles,
     local_tiles,
     w_self,
     bias,
-    dst_rows,
+    push_dst,
     halo_in,
     push_in,
     dst_in,
@@ -55,6 +55,8 @@
     push_buf,
     local_buf,
     base_buf,
+    dst_buf,
+    tile_buf,
     halo_ss,
     halo_rs,
     push_ss,
@@ -68,6 +70,10 @@
     blk = push_tiles.shape[1]
     planes = n // PLANE
     barrier = greet_all(n, me)
+    load_tiles = pltpu.make_async_copy(local_tiles, tile_buf, out_sems.at[2])
+    load_tiles.start()
+    dst_buf[...] = jnp.zeros_like(dst_buf)
+    dst_buf[:, pl.ds(0, n)] = push_dst[...]
 
     def message(i):
         mask = ((i % planes + 1) % planes) * PLANE + i // planes
@@ -93,7 +99,7 @@
 
     def dst_copy(to):
         return pltpu.make_async_remote_copy(
-            dst_rows.at[to], dst_in.at[me], dst_ss, dst_rs, device_id=(to,), device_id_type=MESH
+            dst_buf, dst_in.at[me], dst_ss, dst_rs, device_id=(to,), device_id_type=MESH
         )
 
     def first(i, carry):
@@ -124,18 +130,20 @@
     own = (
         pltpu.make_async_copy(halo_buf.at[me], halo_in.at[me], own_sems.at[0]),
         pltpu.make_async_copy(push_buf.at[me], push_in.at[me], own_sems.at[1]),
-        pltpu.make_async_copy(dst_rows.at[me], dst_in.at[me], own_sems.at[2]),
+        pltpu.make_async_copy(dst_buf, dst_in.at[me], own_sems.at[2]),
     )
     for copy in own:
         copy.start()
 
+    load_tiles.wait()
     slots = local_tiles.shape[1]
 
     def local(b, carry):
         total = jnp.zeros(feats.shape[1:], jnp.float32)
         for j in range(slots):
-            tile = local_tiles[b, j] * keep[b * slots + j].astype(jnp.bfloat16)
-            total += jnp.dot(tile, feats[local_ids[b, j]], preferred_element_type=jnp.float32)
+            live = jnp.minimum(jnp.maximum(local_cnt[b] - j, 0), 1).astype(jnp.float32)
+            tile = tile_buf[b, j] * jnp.full((blk, blk), live, jnp.float32).astype(jnp.bfloat16)
+            total += jnp.dot(tile, feats[local_ids[j, b]], preferred_element_type=jnp.float32)
         rows = pl.ds(pl.multiple_of(b * blk, blk), blk)
         local_buf[rows, :] = total
         base_buf[rows, :] = (
@@ -158,13 +166,13 @@
         (dst_in, dst_rs),
         (halo_buf, halo_ss),
         (push_buf, push_ss),
-        (dst_rows, dst_ss),
+        (dst_in, dst_ss),
     ):
         part = buf.at[pl.ds(0, n - 1)]
         pltpu.make_async_copy(part, part, sem).wait()
 
 
-def exchange(n, send_ids, push_ids, local_ids, keep, feats, push_tiles, local_tiles, w_self, bias, dst_rows):
+def exchange(n, send_ids, push_ids, local_ids, local_cnt, feats, push_tiles, local_tiles, w_self, bias, push_dst):
     blocks, blk, width = feats.shape
     smem = pl.BlockSpec(memory_space=pltpu.SMEM)
     vmem = pl.BlockSpec(memory_space=pltpu.VMEM)
@@ -175,25 +183,27 @@
         out_shape=(
             jax.ShapeDtypeStruct((n, blk, width), jnp.bfloat16),
             jax.ShapeDtypeStruct((n, blk, width), jnp.bfloat16),
-            jax.ShapeDtypeStruct(dst_rows.shape, jnp.int32),
+            jax.ShapeDtypeStruct((n, 1, max(n, 128)), jnp.int32),
             jax.ShapeDtypeStruct((blocks * blk, width), jnp.float32),
             jax.ShapeDtypeStruct((blocks * blk, width), jnp.float32),
         ),
-        in_specs=[smem] * 3 + [vmem] * 7,
+        in_specs=[smem] * 4 + [vmem] * 2 + [hbm] + [vmem] * 3,
         out_specs=(hbm,) * 5,
         scratch_shapes=[
             pltpu.VMEM((n, blk, width), jnp.bfloat16),
             pltpu.VMEM((n, blk, width), jnp.bfloat16),
             pltpu.VMEM((blocks * blk, width), jnp.float32),
             pltpu.VMEM((blocks * blk, width), jnp.float32),
+            pltpu.VMEM((1, max(n, 128)), jnp.int32),
+            pltpu.VMEM(local_tiles.shape, jnp.bfloat16),
         ]
         + [dma] * 6
-        + [dma((3,)), dma((2,))],
+        + [dma((3,)), dma((3,))],
         compiler_params=pltpu.CompilerParams(
             collective_id=0, has_side_effects=True, vmem_limit_bytes=VMEM_BYTES
         ),
         name="exchange",
-    )(send_ids, push_ids, local_ids, keep, feats, push_tiles, local_tiles, w_self, bias, dst_rows)
+    )(send_ids, push_ids, local_ids, local_cnt, feats, push_tiles, local_tiles, w_self, bias, push_dst)
 
 
 def dense_kernel(
@@ -217,6 +227,7 @@
     gb,
 ):
     i = pl.program_id(0)
+    me = lax.axis_index("dom")
     blk = halo_in.shape[1]
     rows, width = feats.shape
 
@@ -232,7 +243,7 @@
             q = i * group + k
             at = pl.ds(pl.multiple_of(halo_dst[q] * blk, blk), blk)
             acc[at, :] += jnp.dot(halo_tiles[k], halo_in[k], preferred_element_type=jnp.float32)
-            at = pl.ds(pl.multiple_of(push_dst[q] * blk, blk), blk)
+            at = pl.ds(pl.multiple_of(push_dst[q, 0, me] * blk, blk), blk)
             acc[at, :] += push_in[k].astype(jnp.float32)
 
     @pl.when(i >= steps)
@@ -443,6 +454,25 @@
     )(term, gbias)
 
 
+def widen_kernel(grads, gbias, grad_self, grad_neigh, grad_bias):
+    width = grad_self.shape[0]
+    grad_self[...] = grads[pl.ds(0, width), :].astype(jnp.float32)
+    grad_neigh[...] = grads[pl.ds(width, width), :].astype(jnp.float32)
+    grad_bias[...] = gbias[pl.ds(0, 1), :]
+
+
+def widen(grads, gbias):
+    vmem = pl.BlockSpec(memory_space=pltpu.VMEM)
+    out = jax.ShapeDtypeStruct((grads.shape[0] // 2, grads.shape[1]), jnp.float32)
+    return pl.pallas_call(
+        widen_kernel,
+        out_shape=(out, out, jax.ShapeDtypeStruct((1, grads.shape[1]), jnp.float32)),
+        in_specs=[vmem, vmem],
+        out_specs=(vmem,) * 3,
+        name="widen",
+    )(grads, gbias)
+
+
 def shards(
     n,
     feats,
@@ -461,25 +491,22 @@
     cotangent,
 ):
     width = feats.shape[1]
-    live = jnp.arange(local_tiles.shape[1])[None, :] < local_cnt[:, None]
-    keep = jnp.broadcast_to(live.astype(jnp.float32).reshape(-1, 1, 1), (live.size, 1, 128))
-    dst_rows = jnp.broadcast_to(push_dst[0][:, None, None], (n, 8, 128))
     halo_in, push_in, dst_in, local_part, base = exchange(
         n,
         halo_send,
         push_src,
-        local_src,
-        keep,
+        local_src.T,
+        local_cnt,
         feats.reshape(-1, push_tiles.shape[2], width),
         push_tiles[0],
         local_tiles,
         w_self,
         bias[None, :],
-        dst_rows,
+        push_dst,
     )
     hidden_out, term, term_bias = dense(
         halo_dst[0],
-        dst_in[:, 0, 0],
+        dst_in,
         halo_in,
         halo_tiles[0],
         push_in,
@@ -490,8 +517,8 @@
         w_neigh,
     )
     grads, gbias = reduce(n, term, term_bias)
-    grads = grads.astype(jnp.float32)
-    return (hidden_out, grads[:width], grads[width:], gbias[0])
+    grad_self, grad_neigh, grad_bias = widen(grads, gbias)
+    return (hidden_out, grad_self, grad_neigh, grad_bias.reshape(width))
 
 
 def solution(mesh):

time: 281 us -> 270 us (0.961)
  local copies, waits for them, and re-layouts: 9.88 us -> 0 us
    slice x3 -> x0, local copies, waits for them, and re-layouts: 6.2 us -> none  [the longest x2 4.1 us: shards(): return (hidden_out, grads[:width], grads[width:], gbias[0])]
    pallas_call x1, Pallas kernels: 196 us -> 192 us  [exchange(): pl.pallas_call(functools.partial(exchange_kernel, n), out_shape=(jax.Shap...]
where the time goes in v2:
time: 270 us; the launch traced here: 269 us
  Pallas kernels  269 us (100%)
    pallas_call x1, Pallas kernels, exchange(): pl.pallas_call(functools.partial(exchange_kernel, n), out_shape=(jax.Shap...  192 us
    pallas_call x1, Pallas kernels, reduce(): pl.pallas_call(functools.partial(reduce_kernel, n), out_shape=(jax.ShapeD...  48.2 us
    pallas_call x1, Pallas kernels, dense(): pl.pallas_call(functools.partial(dense_kernel, steps, group), out_shape=(...  26 us

profile of v2, /device:TPU:0, one launch (start us, length us, event | category | flops | bytes accessed | tf_op | source)
XLA Modules:
  0.0 269.4 jit_solution(13595561588496387038)
XLA Ops:
  0.6 191.9 %exchange.1 = (bf16[32,128,512]{2,1,0:T(8,128)(2,1)}, bf16[32,128,512]{2,1,0:T(8,128)(2,1)}, s32[32,1,128]{2,1,0:T(1,128)}, f32[4096,512]{1,0:T(8,128)}, f32[4096,512]{1,0:T(8,128)}) custom-call(s32[1,32]{1,0:T(1,128)} %send_ids.1, s32[1,32]{1,0:T(1,128)} %push_ids.1, s32[3,32]{1,0:T(4,128)} %bitcast.10, s32[32]{0:T(128)} %local_cnt.1, ...), custom_call_target="tpu_custom_call" | custom-call | tf_op jit(solution)/shard_map/exchange/pallas_call | solution.py:181
  192.6 26.0 %dense.1 = (bf16[4096,512]{1,0:T(8,128)(2,1)}, f32[1024,512]{1,0:T(8,128)}, f32[8,512]{1,0:T(8,128)}) custom-call(s32[32]{0:T(128)} %bitcast.12, s32[32,1,128]{2,1,0:T(1,128)} %get-tuple-element.17.push_dst, bf16[32,128,512]{2,1,0:T(8,128)(2,1)} %get-tuple-element.18.halo_in, bf16[32,128,128]{2,1,0:T(8,128)(2,1)} %bitcast.9, ...), custom_call_target="tpu_custom_call" | custom-call | tf_op jit(solution)/shard_map/dense/pallas_call | solution.py:289
  218.6 48.2 %reduce_grads.1 = (bf16[1024,512]{1,0:T(8,128)(2,1)}, f32[8,512]{1,0:T(8,128)}) custom-call(f32[1024,512]{1,0:T(8,128)} %get-tuple-element.23.term, f32[8,512]{1,0:T(8,128)} %get-tuple-element.24.gbias), custom_call_target="tpu_custom_call" | custom-call | tf_op jit(solution)/shard_map/reduce_grads/pallas_call | solution.py:429
  266.7 2.6 widen.1

commit v3 on v2

--- a/solution.py
+++ b/solution.py
@@ -225,6 +225,8 @@
     acc,
     gt,
     gb,
+    agg_buf,
+    dpre_buf,
 ):
     i = pl.program_id(0)
     me = lax.axis_index("dom")
@@ -246,8 +248,12 @@
             at = pl.ds(pl.multiple_of(push_dst[q, 0, me] * blk, blk), blk)
             acc[at, :] += push_in[k].astype(jnp.float32)
 
-    @pl.when(i >= steps)
-    def _():
+    def gradients():
+        turned = dpre_buf[...].T
+        gt[0] += jnp.dot(turned, feats[...], preferred_element_type=jnp.float32)
+        gt[1] += jnp.dot(turned, agg_buf[...], preferred_element_type=jnp.float32)
+
+    def layer():
         at = pl.ds(pl.multiple_of((i - steps) * rows, rows), rows)
         agg = (acc[at, :] + local_part[...]).astype(jnp.bfloat16)
         pre = base[...] + jnp.dot(agg, w_neigh[...], preferred_element_type=jnp.float32)
@@ -257,9 +263,18 @@
             jnp.bfloat16
         )
         gb[...] += jnp.sum(dpre.astype(jnp.float32).reshape(rows // 8, 8, width), axis=0)
-        turned = dpre.T
-        gt[0] += jnp.dot(turned, feats[...], preferred_element_type=jnp.float32)
-        gt[1] += jnp.dot(turned, agg, preferred_element_type=jnp.float32)
+        agg_buf[...] = agg
+        dpre_buf[...] = dpre
+
+    last = pl.num_programs(0) - 1
+    pl.when(i == steps)(layer)
+
+    @pl.when(jnp.logical_and(i > steps, i < last))
+    def _():
+        gradients()
+        layer()
+
+    pl.when(i == last)(gradients)
 
     @pl.when(i == pl.num_programs(0) - 1)
     def _():
@@ -278,7 +293,10 @@
         return (jnp.minimum(i, steps - 1), 0, 0)
 
     def nodes_at(i, *_):
-        return (jnp.maximum(i - steps, 0), 0)
+        return (jnp.clip(i - steps, 0, chunks - 1), 0)
+
+    def nodes_before(i, *_):
+        return (jnp.maximum(i - steps - 1, 0), 0)
 
     arrived = pl.BlockSpec((group, blk, width), owners)
     chunk = pl.BlockSpec((rows, width), nodes_at)
@@ -295,14 +313,14 @@
         ),
         grid_spec=pltpu.PrefetchScalarGridSpec(
             num_scalar_prefetch=2,
-            grid=(steps + chunks,),
+            grid=(steps + chunks + 1,),
             in_specs=[
                 arrived,
                 pl.BlockSpec((group, blk, blk), owners),
                 arrived,
                 chunk,
                 chunk,
-                chunk,
+                pl.BlockSpec((rows, width), nodes_before),
                 chunk,
                 pl.BlockSpec((width, width), whole),
             ],
@@ -315,6 +333,8 @@
                 pltpu.VMEM((nodes, width), jnp.float32),
                 pltpu.VMEM((2, width, width), jnp.float32),
                 pltpu.VMEM((8, width), jnp.float32),
+                pltpu.VMEM((rows, width), jnp.bfloat16),
+                pltpu.VMEM((rows, width), jnp.bfloat16),
             ],
         ),
         compiler_params=pltpu.CompilerParams(
@@ -324,125 +344,154 @@
     )(halo_dst, push_dst, halo_in, halo_tiles, push_in, local_part, base, feats, cot, w_neigh)
 
 
-def reduce_kernel(
-    n, term, gbias, out, bias_out, acc, send_buf, recv_buf, bias_in, ss, rs, gs, gr, bs, br, own
-):
+def reduce_kernel(n, term, gbias, out, bias_out, acc, send_buf, recv_buf, bias_in, ss, rs, bs, br, own):
     me = lax.axis_index("dom")
     barrier = greet_all(n, me)
-    size = term.shape[0]
+    parts, size, cols = out.shape
+    planes = n // PLANE
+    plane, place = me // PLANE, me % PLANE
     core, second, third = me % 2, (me // 2) % 2, (me // 4) % 2
     bits = [core, second * (1 - core) + third * core, third * (1 - core) + second * core]
     weights = [1, 2 + 2 * core, 4 - 2 * core]
-    weight = 8
-    while weight < n:
-        bits.append((me // weight) % 2)
-        weights.append(weight)
-        weight *= 2
     partners = [me + (1 - 2 * bit) * w for bit, w in zip(bits, weights)]
+    steps = len(bits)
+    sizes = [size // 2 ** (k + 1) for k in range(steps)]
+    bases = [size - 2 * s for s in sizes]
+    starts = [0]
+    for bit, s in zip(bits, sizes):
+        starts.append(starts[-1] + bit * s)
 
     def bias_copy(to):
         return pltpu.make_async_remote_copy(
             gbias, bias_in.at[me], bs, br, device_id=(to,), device_id_type=MESH
         )
 
+    def remote(src, dst, p, k, to):
+        return pltpu.make_async_remote_copy(
+            src, dst, ss.at[p, k], rs.at[p, k], device_id=(to,), device_id_type=MESH
+        )
+
+    def halving(p, k):
+        rows = pl.ds(bases[k], sizes[k])
+        return remote(send_buf.at[p, rows], recv_buf.at[p, rows], p, k, partners[k])
+
+    def value(p, k, off, count):
+        at = pl.ds(pl.multiple_of(starts[k] + off, count), count)
+        if k <= 1:
+            mine = term[at, pl.ds(p * cols, cols)]
+        else:
+            mine = acc[p, at, :]
+        if k == 0:
+            return mine
+        got = pl.ds(pl.multiple_of(bases[k - 1] + off, count), count)
+        return mine + recv_buf[p, got, :].astype(jnp.float32)
+
+    def prepare(p, k):
+        half = sizes[k]
+        send_buf[p, pl.ds(bases[k], half), :] = value(p, k, (1 - bits[k]) * half, half).astype(
+            jnp.bfloat16
+        )
+        if k > 0:
+            at = pl.ds(pl.multiple_of(starts[k + 1], half), half)
+            acc[p, at, :] = value(p, k, bits[k] * half, half)
+
     own_bias = pltpu.make_async_copy(gbias, bias_in.at[me], own)
     own_bias.start()
-    half = size // 2
-    away = pl.multiple_of((1 - bits[0]) * half, half)
-    send_buf[pl.ds(0, half), :] = term[pl.ds(away, half), :].astype(jnp.bfloat16)
+    for p in range(parts):
+        prepare(p, 0)
     pl.semaphore_wait(barrier, n - 1)
-
-    base = 0
-    lo = 0
-    for step, (bit, partner) in enumerate(zip(bits, partners)):
-        half = size // 2
-        copy = pltpu.make_async_remote_copy(
-            send_buf.at[pl.ds(base, half)],
-            recv_buf.at[pl.ds(base, half)],
-            ss.at[step],
-            rs.at[step],
-            device_id=(partner,),
-            device_id_type=MESH,
-        )
-        copy.start()
-        if step == 0:
-
-            def greet(i, carry):
-                bias_copy(lax.rem(me + i, n)).start()
-                return carry
-
-            lax.fori_loop(1, n, greet, 0)
-        lo = lo + bit * half
-        source = term if step == 0 else acc
-        copy.wait()
-        if step + 1 < len(bits):
-            nxt = half // 2
-            bit2 = bits[step + 1]
-            away = (1 - bit2) * nxt
-            at = pl.multiple_of(lo + away, nxt)
-            rel = pl.multiple_of(away, nxt)
-            send_buf[pl.ds(base + half, nxt), :] = (
-                source[pl.ds(at, nxt), :]
-                + recv_buf[pl.ds(pl.multiple_of(base + rel, nxt), nxt), :].astype(jnp.float32)
-            ).astype(jnp.bfloat16)
-            keep = bit2 * nxt
-            at = pl.multiple_of(lo + keep, nxt)
-            acc[pl.ds(at, nxt), :] = source[pl.ds(at, nxt), :] + recv_buf[
-                pl.ds(pl.multiple_of(base + keep, nxt), nxt), :
-            ].astype(jnp.float32)
-        else:
-            at = pl.multiple_of(lo, half)
-            out[pl.ds(at, half), :] = (
-                source[pl.ds(at, half), :] + recv_buf[pl.ds(base, half), :].astype(jnp.float32)
-            ).astype(jnp.bfloat16)
-        base += half
-        size = half
+    for p in range(parts):
+        halving(p, 0).start()
+
+    def greet(i, carry):
+        bias_copy(lax.rem(me + i, n)).start()
+        return carry
+
+    lax.fori_loop(1, n, greet, 0)
+    for k in range(1, steps):
+        for p in range(parts):
+            halving(p, k - 1).wait()
+            prepare(p, k)
+            halving(p, k).start()
+
+    held, lo, last = sizes[-1], starts[-1], bases[-1] + sizes[-1]
+    piece = held // planes
+
+    def scatter(p, h):
+        to = lax.rem(plane + h, planes)
+        src = pl.ds(pl.multiple_of(last + to * piece, piece), piece)
+        dst = pl.ds(pl.multiple_of(last + plane * piece, piece), piece)
+        return remote(send_buf.at[p, src], recv_buf.at[p, dst], p, steps + h - 1, to * PLANE + place)
+
+    for p in range(parts):
+        halving(p, steps - 1).wait()
+        full = value(p, steps, 0, held)
+        send_buf[p, pl.ds(last, held), :] = full.astype(jnp.bfloat16)
+        acc[p, pl.ds(pl.multiple_of(lo, held), held), :] = full
+        for h in range(1, planes):
+            scatter(p, h).start()
+
+    mine = pl.ds(pl.multiple_of(lo + plane * piece, piece), piece)
+
+    def spread(p, h):
+        to = lax.rem(plane + h, planes) * PLANE + place
+        return remote(out.at[p, mine], out.at[p, mine], p, steps + planes - 2 + h, to)
+
+    for p in range(parts):
+        total = acc[p, mine, :]
+        for h in range(1, planes):
+            scatter(p, h).wait()
+        for h in range(1, planes):
+            slot = last + lax.rem(plane + planes - h, planes) * piece
+            total += recv_buf[p, pl.ds(pl.multiple_of(slot, piece), piece), :].astype(jnp.float32)
+        out[p, mine, :] = total.astype(jnp.bfloat16)
+        for h in range(1, planes):
+            spread(p, h).start()
 
     own_bias.wait()
     part = bias_in.at[pl.ds(0, n - 1)]
     pltpu.make_async_copy(part, part, br).wait()
     bias_out[...] = jnp.sum(bias_in[...], axis=0)
 
-    for step in reversed(range(len(bits))):
-        at = pl.ds(pl.multiple_of(lo, size), size)
-        copy = pltpu.make_async_remote_copy(
-            out.at[at],
-            out.at[at],
-            gs.at[step],
-            gr.at[step],
-            device_id=(partners[step],),
-            device_id_type=MESH,
-        )
-        copy.start()
-        copy.wait()
-        lo = lo - bits[step] * size
-        size *= 2
-    part = bias_in.at[pl.ds(0, n - 1)]
+    def doubling(p, k):
+        at = pl.ds(pl.multiple_of(starts[k + 1], sizes[k]), sizes[k])
+        return remote(out.at[p, at], out.at[p, at], p, 2 * (planes - 1) + steps + k, partners[k])
+
+    for p in range(parts):
+        for h in range(1, planes):
+            spread(p, h).wait()
+        doubling(p, steps - 1).start()
+    for k in reversed(range(steps - 1)):
+        for p in range(parts):
+            doubling(p, k + 1).wait()
+            doubling(p, k).start()
+    for p in range(parts):
+        doubling(p, 0).wait()
     pltpu.make_async_copy(part, part, bs).wait()
 
 
 def reduce(n, term, gbias):
     size, width = term.shape
-    steps = n.bit_length() - 1
+    parts = 2
+    copies = 2 * (PLANE.bit_length() - 1 + n // PLANE - 1)
     vmem = pl.BlockSpec(memory_space=pltpu.VMEM)
     dma = pltpu.SemaphoreType.DMA
+    split = (parts, size, width // parts)
     return pl.pallas_call(
         functools.partial(reduce_kernel, n),
         out_shape=(
-            jax.ShapeDtypeStruct((size, width), jnp.bfloat16),
+            jax.ShapeDtypeStruct(split, jnp.bfloat16),
             jax.ShapeDtypeStruct(gbias.shape, jnp.float32),
         ),
         in_specs=[vmem, vmem],
         out_specs=(vmem, vmem),
         scratch_shapes=[
-            pltpu.VMEM((size, width), jnp.float32),
-            pltpu.VMEM((size, width), jnp.bfloat16),
-            pltpu.VMEM((size, width), jnp.bfloat16),
+            pltpu.VMEM(split, jnp.float32),
+            pltpu.VMEM(split, jnp.bfloat16),
+            pltpu.VMEM(split, jnp.bfloat16),
             pltpu.VMEM((n,) + gbias.shape, jnp.float32),
-            dma((steps,)),
-            dma((steps,)),
-            dma((steps,)),
-            dma((steps,)),
+            dma((parts, copies)),
+            dma((parts, copies)),
             dma,
             dma,
             dma,
@@ -456,17 +505,21 @@
 
 def widen_kernel(grads, gbias, grad_self, grad_neigh, grad_bias):
     width = grad_self.shape[0]
-    grad_self[...] = grads[pl.ds(0, width), :].astype(jnp.float32)
-    grad_neigh[...] = grads[pl.ds(width, width), :].astype(jnp.float32)
+    parts, _, cols = grads.shape
+    for p in range(parts):
+        at = pl.ds(p * cols, cols)
+        grad_self[:, at] = grads[p, pl.ds(0, width), :].astype(jnp.float32)
+        grad_neigh[:, at] = grads[p, pl.ds(width, width), :].astype(jnp.float32)
     grad_bias[...] = gbias[pl.ds(0, 1), :]
 
 
 def widen(grads, gbias):
     vmem = pl.BlockSpec(memory_space=pltpu.VMEM)
-    out = jax.ShapeDtypeStruct((grads.shape[0] // 2, grads.shape[1]), jnp.float32)
+    width = gbias.shape[1]
+    out = jax.ShapeDtypeStruct((grads.shape[1] // 2, width), jnp.float32)
     return pl.pallas_call(
         widen_kernel,
-        out_shape=(out, out, jax.ShapeDtypeStruct((1, grads.shape[1]), jnp.float32)),
+        out_shape=(out, out, jax.ShapeDtypeStruct((1, width), jnp.float32)),
         in_specs=[vmem, vmem],
         out_specs=(vmem,) * 3,
         name="widen",

time: 270 us -> 260 us (0.963)
  Pallas kernels: 269 us -> 259 us
    pallas_call x1, Pallas kernels: 48.2 us -> 38.5 us  [reduce(): pl.pallas_call(functools.partial(reduce_kernel, n), out_shape=(jax.ShapeD...]
where the time goes in v3:
time: 260 us
  Pallas kernels  259 us (100%)
    pallas_call x1, Pallas kernels, exchange(): pl.pallas_call(functools.partial(exchange_kernel, n), out_shape=(jax.Shap...  192 us
    pallas_call x1, Pallas kernels, reduce(): pl.pallas_call(functools.partial(reduce_kernel, n), out_shape=(jax.ShapeD...  38.5 us
    pallas_call x1, Pallas kernels, dense(): pl.pallas_call(functools.partial(dense_kernel, steps, group), out_shape=(...  25.9 us

profile of v3, /device:TPU:0, one launch (start us, length us, event | category | flops | bytes accessed | tf_op | source)
XLA Modules:
  0.0 259.7 jit_solution(9593748768788247169)
XLA Ops:
  0.6 191.9 %exchange.1 = (bf16[32,128,512]{2,1,0:T(8,128)(2,1)}, bf16[32,128,512]{2,1,0:T(8,128)(2,1)}, s32[32,1,128]{2,1,0:T(1,128)}, f32[4096,512]{1,0:T(8,128)}, f32[4096,512]{1,0:T(8,128)}) custom-call(s32[1,32]{1,0:T(1,128)} %send_ids.1, s32[1,32]{1,0:T(1,128)} %push_ids.1, s32[3,32]{1,0:T(4,128)} %bitcast.10, s32[32]{0:T(128)} %local_cnt.1, ...), custom_call_target="tpu_custom_call" | custom-call | tf_op jit(solution)/shard_map/exchange/pallas_call | solution.py:181
  192.6 25.9 %dense.1 = (bf16[4096,512]{1,0:T(8,128)(2,1)}, f32[1024,512]{1,0:T(8,128)}, f32[8,512]{1,0:T(8,128)}) custom-call(s32[32]{0:T(128)} %bitcast.12, s32[32,1,128]{2,1,0:T(1,128)} %get-tuple-element.17.push_dst, bf16[32,128,512]{2,1,0:T(8,128)(2,1)} %get-tuple-element.18.halo_in, bf16[32,128,128]{2,1,0:T(8,128)(2,1)} %bitcast.9, ...), custom_call_target="tpu_custom_call" | custom-call | tf_op jit(solution)/shard_map/dense/pallas_call | solution.py:307
  218.5 38.5 %reduce_grads.1 = (bf16[2,1024,256]{2,1,0:T(8,128)(2,1)}, f32[8,512]{1,0:T(8,128)}) custom-call(f32[1024,512]{1,0:T(8,128)} %get-tuple-element.23.term, f32[8,512]{1,0:T(8,128)} %get-tuple-element.24.gbias), custom_call_target="tpu_custom_call" | custom-call | tf_op jit(solution)/shard_map/reduce_grads/pallas_call | solution.py:480
  257.0 2.6 %widen.1 = (f32[512,512]{1,0:T(8,128)}, f32[512,512]{1,0:T(8,128)}, f32[1,512]{1,0:T(1,128)}) custom-call(bf16[2,1024,256]{2,1,0:T(8,128)(2,1)} %get-tuple-element.25.grads, f32[8,512]{1,0:T(8,128)} %get-tuple-element.26.gbias), custom_call_target="tpu_custom_call" | custom-call | tf_op jit(solution)/shard_map/widen/pallas_call | solution.py:520

commit v4 on v3

--- a/solution.py
+++ b/solution.py
@@ -286,7 +286,7 @@
 def dense(halo_dst, push_dst, halo_in, halo_tiles, push_in, local_part, base, feats, cot, w_neigh):
     n, blk, width = halo_in.shape
     nodes = feats.shape[0]
-    group, rows = 4, 512
+    group, rows = 8, 1024
     steps, chunks = n // group, nodes // rows
 
     def owners(i, *_):
@@ -472,7 +472,7 @@
 
 def reduce(n, term, gbias):
     size, width = term.shape
-    parts = 2
+    parts = 4
     copies = 2 * (PLANE.bit_length() - 1 + n // PLANE - 1)
     vmem = pl.BlockSpec(memory_space=pltpu.VMEM)
     dma = pltpu.SemaphoreType.DMA

time: 260 us -> 256 us (0.985)
  Pallas kernels: 259 us -> 255 us
    pallas_call x1, Pallas kernels: 25.9 us -> 23.2 us  [dense(): pl.pallas_call(functools.partial(dense_kernel, steps, group), out_shape=(...]
where the time goes in v4:
time: 256 us; the launch traced here: 255 us
  Pallas kernels  255 us (100%)
    pallas_call x1, Pallas kernels, exchange(): pl.pallas_call(functools.partial(exchange_kernel, n), out_shape=(jax.Shap...  192 us
    pallas_call x1, Pallas kernels, reduce(): pl.pallas_call(functools.partial(reduce_kernel, n), out_shape=(jax.ShapeD...  36.8 us
    pallas_call x1, Pallas kernels, dense(): pl.pallas_call(functools.partial(dense_kernel, steps, group), out_shape=(...  23.2 us

profile of v4, /device:TPU:0, one launch (start us, length us, event | category | flops | bytes accessed | tf_op | source)
XLA Modules:
  0.0 255.3 jit_solution(17644671209415944684)
XLA Ops:
  0.6 191.9 %exchange.1 = (bf16[32,128,512]{2,1,0:T(8,128)(2,1)}, bf16[32,128,512]{2,1,0:T(8,128)(2,1)}, s32[32,1,128]{2,1,0:T(1,128)}, f32[4096,512]{1,0:T(8,128)}, f32[4096,512]{1,0:T(8,128)}) custom-call(s32[1,32]{1,0:T(1,128)} %send_ids.1, s32[1,32]{1,0:T(1,128)} %push_ids.1, s32[3,32]{1,0:T(4,128)} %bitcast.10, s32[32]{0:T(128)} %local_cnt.1, ...), custom_call_target="tpu_custom_call" | custom-call | tf_op jit(solution)/shard_map/exchange/pallas_call | solution.py:181
  192.6 23.2 %dense.1 = (bf16[4096,512]{1,0:T(8,128)(2,1)}, f32[1024,512]{1,0:T(8,128)}, f32[8,512]{1,0:T(8,128)}) custom-call(s32[32]{0:T(128)} %bitcast.12, s32[32,1,128]{2,1,0:T(1,128)} %get-tuple-element.17.push_dst, bf16[32,128,512]{2,1,0:T(8,128)(2,1)} %get-tuple-element.18.halo_in, bf16[32,128,128]{2,1,0:T(8,128)(2,1)} %bitcast.9, ...), custom_call_target="tpu_custom_call" | custom-call | tf_op jit(solution)/shard_map/dense/pallas_call | solution.py:307
  215.7 36.8 %reduce_grads.1 = (bf16[4,1024,128]{2,1,0:T(8,128)(2,1)}, f32[8,512]{1,0:T(8,128)}) custom-call(f32[1024,512]{1,0:T(8,128)} %get-tuple-element.23.term, f32[8,512]{1,0:T(8,128)} %get-tuple-element.24.gbias), custom_call_target="tpu_custom_call" | custom-call | tf_op jit(solution)/shard_map/reduce_grads/pallas_call | solution.py:480
  252.6 2.7 %widen.1 = (f32[512,512]{1,0:T(8,128)}, f32[512,512]{1,0:T(8,128)}, f32[1,512]{1,0:T(1,128)}) custom-call(bf16[4,1024,128]{2,1,0:T(8,128)(2,1)} %get-tuple-element.25.grads, f32[8,512]{1,0:T(8,128)} %get-tuple-element.26.gbias), custom_call_target="tpu_custom_call" | custom-call | tf_op jit(solution)/shard_map/widen/pallas_call | solution.py:520
